TPU v7x, 32 devices: a whole 2x2x4 slice. The times are simulated.
32 devices in a mesh: dp: 8 (over z, x), seq: 4 (over y, core).
Axes of the slice: x: 2, y: 2, z: 4, core: 2. Of those that a mesh axis runs over, the one named last changes fastest.
Arguments:
- tokens: bfloat16 [16384, 1024], P(('dp', 'seq')), may hold values from -6 to 6
- time_embed: bfloat16 [32, 1024], P(('dp', 'seq')), may hold values from -6 to 6
- lengths: int32 [32], P('dp'), may hold values from 0 to 475, as said below
- cotangent: bfloat16 [16384, 1024], P(('dp', 'seq')), may hold values from -6 to 6
- w_query: bfloat16 [1024, 1024], P('seq'), may hold values from -0.1875 to 0.1875
- w_key: bfloat16 [1024, 1024], P('seq'), may hold values from -0.1875 to 0.1875
- w_value: bfloat16 [1024, 1024], P('seq'), may hold values from -0.1875 to 0.1875
- w_out: bfloat16 [1024, 1024], P('seq'), may hold values from -0.75 to 0.75
- w_time: bfloat16 [1024, 1024], P('seq'), may hold values from -0.1875 to 0.1875
- w_in: bfloat16 [4096, 1024], P('seq'), may hold values from -0.1875 to 0.1875
- w_down: bfloat16 [4096, 1024], P('seq'), may hold values from -0.09375 to 0.09375
- b_query: bfloat16 [1024], replicated, may hold values from -3 to 3
- b_value: bfloat16 [1024], replicated, may hold values from -3 to 3
- b_out: bfloat16 [1024], replicated, may hold values from -3 to 3
- b_time: bfloat16 [1024], replicated, may hold values from -3 to 3
- b_in: bfloat16 [4096], replicated, may hold values from -3 to 3
- b_down: bfloat16 [1024], replicated, may hold values from -2 to 2
- gain_one: bfloat16 [1024], replicated, may hold values from 0.25 to 1.75
- shift_one: bfloat16 [1024], replicated, may hold values from -2 to 2
- gain_two: bfloat16 [1024], replicated, may hold values from 0.25 to 1.75
- shift_two: bfloat16 [1024], replicated, may hold values from -2 to 2
Outputs:
- layer_out: bfloat16 [16384, 1024], P(('dp', 'seq'))
- grad_tokens: bfloat16 [16384, 1024], P(('dp', 'seq'))
- grad_w_query: float32 [1024, 1024], P('seq')
- grad_w_key: float32 [1024, 1024], P('seq')
- grad_w_value: float32 [1024, 1024], P('seq')
- grad_w_out: float32 [1024, 1024], P('seq')
- grad_w_time: float32 [1024, 1024], P('seq')
- grad_w_in: float32 [4096, 1024], P('seq')
- grad_w_down: float32 [4096, 1024], P('seq')
- grad_b_query: float32 [1024], replicated
- grad_b_value: float32 [1024], replicated
- grad_b_out: float32 [1024], replicated
- grad_b_time: float32 [1024], replicated
- grad_b_in: float32 [4096], replicated
- grad_b_down: float32 [1024], replicated
- grad_gain_one: float32 [1024], replicated
- grad_shift_one: float32 [1024], replicated
- grad_gain_two: float32 [1024], replicated
- grad_shift_two: float32 [1024], replicated
Inputs may be any that keep to these rules, and one draw needn't show every extreme that they name: Item i's valid slots are its first lengths[i] + 25; every draw has an item of length 475 and one of length 0.
All inputs are finite; a program needn't handle non-finite values.
Results may differ from a plain program's by a relative error of at most 0.02.
Values may be sent and summed in bfloat16 or wider, within the bound.
A program may use at most 256 MiB of HBM per device.

v0:
```python
import jax
import jax.numpy as jnp
from jax import lax
from jax.sharding import PartitionSpec as P

HEAD_DIM = 64
BLOCK = 25
norm_eps = 1e-05
neg_large = -1e30


def layer_norm(values, gain, shift):
    center = values - jnp.mean(values, axis=-1, keepdims=True)
    spread = lax.rsqrt(jnp.mean(center * center, axis=-1, keepdims=True) + norm_eps)
    return center * spread * gain + shift


def exact_gelu(values):
    return jax.nn.gelu(values, approximate=False)


def split_heads(rows):
    return rows.reshape(rows.shape[0], rows.shape[1] // HEAD_DIM, HEAD_DIM)


def item_scores(item_block, key_valid):
    queries = split_heads(item_block[:, 0])
    key_heads = split_heads(item_block[:, 1])
    value_heads = split_heads(item_block[:, 2])
    scores = jnp.einsum(
        "qhd,khd->hqk", queries, key_heads, preferred_element_type=jnp.float32
    ) * HEAD_DIM ** (-0.5)
    masked = jnp.where(key_valid[None, None, :], scores, neg_large)
    return (queries, key_heads, value_heads, masked)


def attend_forward(packed):
    item_block, key_valid = packed
    queries, key_heads, value_heads, masked = item_scores(item_block, key_valid)
    row_max = jnp.max(masked, axis=-1, keepdims=True)
    exp_scores = jnp.exp(masked - row_max)
    row_total = jnp.sum(exp_scores, axis=-1, keepdims=True)
    soft_weights = (exp_scores / row_total).astype(jnp.bfloat16)
    mixed_heads = jnp.einsum(
        "hqk,khd->qhd", soft_weights, value_heads, preferred_element_type=jnp.float32
    )
    log_total = row_max[:, :, 0] + jnp.log(row_total[:, :, 0])
    return (mixed_heads.reshape(item_block.shape[0], -1).astype(jnp.bfloat16), log_total)


def attend_backward(packed):
    item_block, key_valid, log_total, grad_block = packed
    queries, key_heads, value_heads, masked = item_scores(item_block, key_valid)
    soft_weights = jnp.exp(masked - log_total[:, :, None])
    grad_heads = split_heads(grad_block)
    grad_value = jnp.einsum(
        "hqk,qhd->khd",
        soft_weights.astype(jnp.bfloat16),
        grad_heads,
        preferred_element_type=jnp.float32,
    )
    grad_soft = jnp.einsum(
        "qhd,khd->hqk", grad_heads, value_heads, preferred_element_type=jnp.float32
    )
    grad_scores = soft_weights * (
        grad_soft - jnp.sum(soft_weights * grad_soft, axis=-1, keepdims=True)
    )
    scores_low = grad_scores.astype(jnp.bfloat16)
    score_scale = HEAD_DIM ** (-0.5)
    grad_query = (
        jnp.einsum("hqk,khd->qhd", scores_low, key_heads, preferred_element_type=jnp.float32)
        * score_scale
    )
    grad_key = (
        jnp.einsum("hqk,qhd->khd", scores_low, queries, preferred_element_type=jnp.float32)
        * score_scale
    )
    slot_count = item_block.shape[0]
    return jnp.stack(
        [
            grad_query.reshape(slot_count, -1),
            grad_key.reshape(slot_count, -1),
            grad_value.reshape(slot_count, -1),
        ],
        axis=1,
    ).astype(jnp.bfloat16)


def local(
    tokens,
    time_embed,
    lengths,
    cotangent,
    w_query,
    w_key,
    w_value,
    w_out,
    w_time,
    w_in,
    w_down,
    b_query,
    b_value,
    b_out,
    b_time,
    b_in,
    b_down,
    gain_one,
    shift_one,
    gain_two,
    shift_two,
):
    seq_rank = lax.axis_index("seq")
    item_count = time_embed.shape[0]
    token_count = tokens.shape[0]
    slot_count = token_count // item_count
    model_width = tokens.shape[1]
    full_query, full_key, full_value, full_out, full_time, full_in, full_down = (
        lax.all_gather(w_query, "seq", axis=0, tiled=True),
        lax.all_gather(w_key, "seq", axis=0, tiled=True),
        lax.all_gather(w_value, "seq", axis=0, tiled=True),
        lax.all_gather(w_out, "seq", axis=0, tiled=True),
        lax.all_gather(w_time, "seq", axis=0, tiled=True),
        lax.all_gather(w_in, "seq", axis=0, tiled=True),
        lax.all_gather(w_down, "seq", axis=0, tiled=True),
    )
    bias_query = b_query.astype(jnp.float32)
    bias_value = b_value.astype(jnp.float32)
    bias_out = b_out.astype(jnp.float32)
    bias_time = b_time.astype(jnp.float32)
    bias_in = b_in.astype(jnp.float32)
    bias_down = b_down.astype(jnp.float32)
    gain_first = gain_one.astype(jnp.float32)
    shift_first = shift_one.astype(jnp.float32)
    gain_last = gain_two.astype(jnp.float32)
    shift_last = shift_two.astype(jnp.float32)
    slot_index = lax.broadcasted_iota(jnp.int32, (lengths.shape[0], slot_count), 1)
    group_valid = slot_index < lengths[:, None] + BLOCK
    own_valid = lax.dynamic_slice_in_dim(group_valid, seq_rank * item_count, item_count, 0)
    row_keep = own_valid.reshape(token_count, 1).astype(jnp.float32)
    time_proj = jnp.dot(time_embed, full_time, preferred_element_type=jnp.float32) + bias_time
    resid = (tokens.reshape(item_count, slot_count, model_width) + time_proj[:, None, :]).reshape(
        token_count, model_width
    )
    resid_low = resid.astype(jnp.bfloat16)
    query_rows = (
        jnp.dot(resid_low, full_query, preferred_element_type=jnp.float32) + bias_query
    ).astype(jnp.bfloat16)
    key_rows = jnp.dot(resid_low, full_key, preferred_element_type=jnp.float32).astype(jnp.bfloat16)
    value_rows = (
        jnp.dot(resid_low, full_value, preferred_element_type=jnp.float32) + bias_value
    ).astype(jnp.bfloat16)
    stacked = jnp.stack([query_rows, key_rows, value_rows], axis=1).reshape(
        item_count, slot_count, 3, model_width
    )
    head_side = lax.all_to_all(stacked, "seq", split_axis=3, concat_axis=0, tiled=True)
    mixed_heads, log_totals = lax.map(attend_forward, (head_side, group_valid))
    mixed_rows = lax.all_to_all(
        mixed_heads, "seq", split_axis=0, concat_axis=2, tiled=True
    ).reshape(token_count, model_width)
    attn_out = jnp.dot(mixed_rows, full_out, preferred_element_type=jnp.float32) + bias_out
    first_norm, first_pull = jax.vjp(layer_norm, resid + attn_out, gain_first, shift_first)
    first_low = first_norm.astype(jnp.bfloat16)
    hidden_pre = (
        jnp.einsum("td,fd->tf", first_low, full_in, preferred_element_type=jnp.float32) + bias_in
    )
    hidden, gelu_pull = jax.vjp(exact_gelu, hidden_pre)
    hidden_low = hidden.astype(jnp.bfloat16)
    ffn_out = jnp.dot(hidden_low, full_down, preferred_element_type=jnp.float32) + bias_down
    second_norm, second_pull = jax.vjp(layer_norm, first_norm + ffn_out, gain_last, shift_last)
    layer_out = (second_norm * row_keep).astype(jnp.bfloat16)
    back_query, back_key, back_value, back_out, back_in, back_down = (
        lax.all_gather(w_query, "seq", axis=0, tiled=True),
        lax.all_gather(w_key, "seq", axis=0, tiled=True),
        lax.all_gather(w_value, "seq", axis=0, tiled=True),
        lax.all_gather(w_out, "seq", axis=0, tiled=True),
        lax.all_gather(w_in, "seq", axis=0, tiled=True),
        lax.all_gather(w_down, "seq", axis=0, tiled=True),
    )
    grad_second_in, grad_gain_two, grad_shift_two = second_pull(
        cotangent.astype(jnp.float32) * row_keep
    )
    grad_ffn = grad_second_in.astype(jnp.bfloat16)
    grad_hidden = jnp.einsum("td,fd->tf", grad_ffn, back_down, preferred_element_type=jnp.float32)
    grad_pre = gelu_pull(grad_hidden)[0].astype(jnp.bfloat16)
    grad_first = grad_second_in + jnp.dot(grad_pre, back_in, preferred_element_type=jnp.float32)
    grad_first_in, grad_gain_one, grad_shift_one = first_pull(grad_first)
    grad_attn = grad_first_in.astype(jnp.bfloat16)
    grad_mixed = jnp.einsum(
        "td,ed->te", grad_attn, back_out, preferred_element_type=jnp.float32
    ).astype(jnp.bfloat16)
    grad_heads = lax.all_to_all(
        grad_mixed.reshape(item_count, slot_count, model_width),
        "seq",
        split_axis=2,
        concat_axis=0,
        tiled=True,
    )
    grad_stack = lax.map(attend_backward, (head_side, group_valid, log_totals, grad_heads))
    grad_qkv = lax.all_to_all(grad_stack, "seq", split_axis=0, concat_axis=3, tiled=True).reshape(
        token_count, 3, model_width
    )
    grad_query_rows = grad_qkv[:, 0]
    grad_key_rows = grad_qkv[:, 1]
    grad_value_rows = grad_qkv[:, 2]
    grad_resid = grad_first_in + jnp.einsum(
        "te,de->td", grad_query_rows, back_query, preferred_element_type=jnp.float32
    )
    grad_resid = grad_resid + jnp.einsum(
        "te,de->td", grad_key_rows, back_key, preferred_element_type=jnp.float32
    )
    grad_resid = grad_resid + jnp.einsum(
        "te,de->td", grad_value_rows, back_value, preferred_element_type=jnp.float32
    )
    grad_tokens = grad_resid.astype(jnp.bfloat16)
    grad_time = jnp.sum(grad_resid.reshape(item_count, slot_count, model_width), axis=1).astype(
        jnp.bfloat16
    )
    term_in = jnp.einsum("tf,td->fd", grad_pre, first_low, preferred_element_type=jnp.float32)
    term_down = jnp.einsum("tf,td->fd", hidden_low, grad_ffn, preferred_element_type=jnp.float32)
    ffn_share = lax.psum_scatter(
        jnp.concatenate([term_in, term_down], axis=1).astype(jnp.bfloat16),
        "seq",
        scatter_dimension=0,
        tiled=True,
    ).astype(jnp.float32)
    share_in = ffn_share[:, :model_width]
    share_down = ffn_share[:, model_width:]
    grad_qkv_flat = grad_qkv.reshape(token_count, 3 * model_width)
    term_qkv = jnp.einsum("tr,te->re", resid_low, grad_qkv_flat, preferred_element_type=jnp.float32)
    term_out = jnp.einsum("tr,te->re", mixed_rows, grad_attn, preferred_element_type=jnp.float32)
    term_time = jnp.einsum("tr,te->re", time_embed, grad_time, preferred_element_type=jnp.float32)
    attn_share = lax.psum_scatter(
        jnp.concatenate([term_qkv, term_out, term_time], axis=1).astype(jnp.bfloat16),
        "seq",
        scatter_dimension=0,
        tiled=True,
    ).astype(jnp.float32)
    sum_in, sum_down, sum_attn = lax.psum((share_in, share_down, attn_share), "dp")
    (
        grad_b_query,
        grad_b_value,
        grad_b_out,
        grad_b_time,
        grad_b_in,
        grad_b_down,
        sum_gain_one,
        sum_shift_one,
        sum_gain_two,
        sum_shift_two,
    ) = lax.psum(
        (
            jnp.sum(grad_query_rows, axis=0, dtype=jnp.float32),
            jnp.sum(grad_value_rows, axis=0, dtype=jnp.float32),
            jnp.sum(grad_attn, axis=0, dtype=jnp.float32),
            jnp.sum(grad_time, axis=0, dtype=jnp.float32),
            jnp.sum(grad_pre, axis=0, dtype=jnp.float32),
            jnp.sum(grad_ffn, axis=0, dtype=jnp.float32),
            grad_gain_one,
            grad_shift_one,
            grad_gain_two,
            grad_shift_two,
        ),
        ("dp", "seq"),
    )
    return (
        layer_out,
        grad_tokens,
        sum_attn[:, :model_width],
        sum_attn[:, model_width : 2 * model_width],
        sum_attn[:, 2 * model_width : 3 * model_width],
        sum_attn[:, 3 * model_width : 4 * model_width],
        sum_attn[:, 4 * model_width :],
        sum_in,
        sum_down,
        grad_b_query,
        grad_b_value,
        grad_b_out,
        grad_b_time,
        grad_b_in,
        grad_b_down,
        sum_gain_one,
        sum_shift_one,
        sum_gain_two,
        sum_shift_two,
    )


def solution(mesh):
    in_specs = (
        P(("dp", "seq"), None),
        P(("dp", "seq"), None),
        P("dp"),
        P(("dp", "seq"), None),
        P("seq", None),
        P("seq", None),
        P("seq", None),
        P("seq", None),
        P("seq", None),
        P("seq", None),
        P("seq", None),
        P(),
        P(),
        P(),
        P(),
        P(),
        P(),
        P(),
        P(),
        P(),
        P(),
    )
    out_specs = (
        P(("dp", "seq"), None),
        P(("dp", "seq"), None),
        P("seq", None),
        P("seq", None),
        P("seq", None),
        P("seq", None),
        P("seq", None),
        P("seq", None),
        P("seq", None),
        P(),
        P(),
        P(),
        P(),
        P(),
        P(),
        P(),
        P(),
        P(),
        P(),
    )
    return jax.shard_map(local, mesh=mesh, in_specs=in_specs, out_specs=out_specs, check_vma=False)
```

profile of v0, /device:TPU:0, one launch (start us, length us, event | category | flops | bytes accessed | tf_op | source)
XLA Modules:
  0.0 1024.9 jit_solution(11175937221474394372)
XLA Ops:
  11.2 23.7 %all-gather.8.cloned.1.call-done = bf16[1024,1024]{1,0:T(8,128)(2,1)} async-done(((bf16[256,1024]{1,0:T(8,128)(2,1)}), bf16[1024,1024]{1,0:T(8,128)(2,1)}) %all-gather.8.cloned.1.call-update) | async-done | bytes 2097168 | tf_op jit(solution)/shard_map/all_gather | solution.py:122
  36.9 22.2 %all-gather.12.cloned.1.call-done = bf16[1024,1024]{1,0:T(8,128)(2,1)} async-done(((bf16[256,1024]{1,0:T(8,128)(2,1)}), bf16[1024,1024]{1,0:T(8,128)(2,1)}) %all-gather.12.cloned.1.call-update) | async-done | bytes 2097168 | tf_op jit(solution)/shard_map/all_gather | solution.py:119
  62.9 20.3 %all-gather.10.cloned.1.call-done = bf16[1024,1024]{1,0:T(8,128)(2,1)} async-done(((bf16[256,1024]{1,0:T(8,128)(2,1)}), bf16[1024,1024]{1,0:T(8,128)(2,1)}) %all-gather.10.cloned.1.call-update) | async-done | bytes 2097168 | tf_op jit(solution)/shard_map/all_gather | solution.py:118
  87.1 20.2 %all-gather.14.cloned.1.call-done = bf16[1024,1024]{1,0:T(8,128)(2,1)} async-done(((bf16[256,1024]{1,0:T(8,128)(2,1)}), bf16[1024,1024]{1,0:T(8,128)(2,1)}) %all-gather.14.cloned.1.call-update) | async-done | bytes 2097168 | tf_op jit(solution)/shard_map/all_gather | solution.py:120
  110.6 5.7 copy.80
  116.3 5.1 all-to-all-start
  122.3 77.5 %all-to-all-done = bf16[1,512,3,1024]{1,2,0,3:T(4,128)(2,1)} async-done(((bf16[1,512,3,1024]{1,2,0,3:T(4,128)(2,1)}), bf16[1,512,3,1024]{1,2,0,3:T(4,128)(2,1)}, u32[]{:S(2)}, u32[]{:S(2)}) %all-to-all-start) | async-done | bytes 3145760 | tf_op jit(solution)/shard_map/all_to_all | solution.py:155
  202.9 16.3 %while.22 = (s32[]{:T(128)}, bf16[4,512,256]{1,2,0:T(8,128)(2,1)}, f32[4,4,512]{2,1,0:T(4,128)S(1)}, bf16[4,512,3,256]{1,3,2,0:T(8,128)(2,1)S(1)}, pred[4,512]{1,0:T(4,128)(4,1)S(1)}, /*index=5*/s32[]{:T(128)}) while((s32[]{:T(128)}, bf16[4,512,256]{1,2,0:T(8,128)(2,1)}, f32[4,4,512]{2,1,0:T(4,128)S(1)}, ...), condition=%wide.region_3.4_spmd, body=%wide.region_0.3_spmd.sunk | while | flops 281147392 | bytes 17370192 | solution.py:156
  223.7 18.0 %all-to-all-done.1 = bf16[4,512,256]{1,2,0:T(8,128)(2,1)} async-done(((bf16[4,512,256]{1,2,0:T(8,128)(2,1)}), bf16[4,512,256]{1,2,0:T(8,128)(2,1)}, u32[]{:S(2)}, u32[]{:S(2)}) %all-to-all-start.1) | async-done | bytes 1048608 | tf_op jit(solution)/shard_map/all_to_all | solution.py:157
  247.0 27.2 %multiply_convert_fusion.1 = (bf16[512,4096]{1,0:T(8,128)(2,1)}, f32[512,4096]{1,0:T(8,128)}, f32[512,4096]{1,0:T(8,128)}) fusion(f32[4096]{0:T(1024)S(1)} %convert_element_type.170, bf16[4096,1024]{1,0:T(8,128)(2,1)} %all-gather.18.cloned.1.call-done, f32[512,1024]{1,0:T(8,128)} %copy-done, f32[1024]{0:T(1024)S(1)} %convert_element_type.168, ...), kind=kOutput, calls=%fused_computation.37 | convolution fusion | flops 4436000768 | bytes 31485952 | tf_op jit(solution)/shard_map/td,fd->tf/dot_general | solution.py:164
  274.2 10.3 %all-gather.20.cloned.1.call-done = bf16[4096,1024]{1,0:T(8,128)(2,1)} async-done(((bf16[1024,1024]{1,0:T(8,128)(2,1)}), bf16[4096,1024]{1,0:T(8,128)(2,1)}) %all-gather.20.cloned.1.call-update) | async-done | bytes 8388624 | tf_op jit(solution)/shard_map/all_gather | solution.py:124
  284.5 10.0 fusion.59
  300.6 7.1 convolution_convert_fusion
  307.7 13.5 %convert_reduce_fusion = (f32[4096]{0:T(1024)S(1)}, bf16[512,4096]{1,0:T(8,128)(2,1)S(1)}) fusion(f32[512,4096]{1,0:T(8,128)} %get-tuple-element.209, f32[512,4096]{1,0:T(8,128)} %get-tuple-element.234, f32[4096]{0:T(1024)S(1)} %convert_element_type.170, bf16[512,1024]{1,0:T(8,128)(2,1)S(1)} %get-tuple-element.199, ...), kind=kOutput, calls=%fused_computation.35 | convolution fusion | flops 4330614784 | bytes 30441472 | tf_op jit(solution)/shard_map/td,fd->tf/dot_general | solution.py:183
  321.3 7.0 convolution_convert_fusion.1
  328.3 13.9 %pad_maximum_fusion = bf16[4096,2048]{0,1:T(8,128)(2,1)} fusion(bf16[4096,1024]{0,1:T(8,128)(2,1)} %convolution_convert_fusion, bf16[4096,1024]{0,1:T(8,128)(2,1)} %convolution_convert_fusion.1), kind=kLoop, calls=%fused_computation.31 | loop fusion | flops 33554432 | bytes 33554432 | tf_op jit(solution)/shard_map/concatenate | solution.py:221
  342.2 11.4 %multiply_reduce_fusion.2 = (f32[1024]{0:T(1024)S(1)}, f32[512]{0:T(512)S(1)}, f32[1024]{0:T(1024)S(1)}, f32[512,1024]{1,0:T(8,128)S(1)}) fusion(f32[512,1024]{1,0:T(8,128)} %copy-done, f32[512]{0:T(512)S(1)} %fusion.42, f32[512]{0:T(512)S(1)} %broadcast_multiply_fusion.1, f32[1024]{0:T(1024)S(1)} %convert_element_type.167, ...), kind=kOutput, calls=%fused_computation.61 | convolution fusion | flops 4300207616 | bytes 18894848 | tf_op jit(solution)/shard_map/dot_general | solution.py:185
  359.2 6.2 copy.82
  365.9 9.0 reduce.7
  378.8 4.3 all-to-all-start.2
  383.1 26.1 %all-to-all-done.2 = bf16[4,2,65536]{2,1,0:T(2,128)(2,1)} async-done(((bf16[4,2,65536]{2,1,0:T(2,128)(2,1)}), bf16[4,2,65536]{2,1,0:T(2,128)(2,1)}, u32[]{:S(2)}, u32[]{:S(2)}) %all-to-all-start.2) | async-done | bytes 1048608 | tf_op jit(solution)/shard_map/all_to_all | solution.py:191
  416.1 35.0 %while.23 = (s32[]{:T(128)}, bf16[4,512,3,256]{1,3,2,0:T(8,128)(2,1)}, bf16[4,512,3,256]{1,3,2,0:T(8,128)(2,1)S(1)}, pred[4,512]{1,0:T(4,128)(4,1)S(1)}, f32[4,4...) while((s32[]{:T(128)}, bf16[4,512,3,256]{1,3,2,0:T(8,128)(2,1)}, ...), condition=%wide.region_14.15_spmd, body=%wide.region_12.14_spmd.sunk | while | flops 689829888 | bytes 39382108 | solution.py:198
  459.2 51.5 %all-to-all-done.3 = bf16[4,512,3,256]{1,3,2,0:T(8,128)(2,1)S(1)} async-done(((bf16[4,512,3,256]{1,3,2,0:T(8,128)(2,1)}), bf16[4,512,3,256]{1,3,2,0:T(8,128)(2,1)S(1)}, u32[]{:S(2)}, u32[]{:S(2)}) %all-to-all-start.3) | async-done | bytes 3145760 | tf_op jit(solution)/shard_map/all_to_all | solution.py:199
  524.0 9.9 pad_maximum_fusion.1
  534.0 6.8 fusion.55
  548.6 41.3 %all-reduce = (f32[1024]{0:T(1024)}, f32[1024]{0:T(1024)}, f32[1024]{0:T(1024)}, f32[1024]{0:T(1024)}, f32[4096]{0:T(1024)}, /*index=5*/f32[1024]{0:T(1024)}, f3...) all-reduce(f32[1024]{0:T(1024)S(1)} %get-tuple-element.240, ...), channel_id=1, replica_groups=mesh['dp'=8,'seq'=4] {'dp','seq'}, use_global_device_ids=true, to_apply=%region_22.23 | all-reduce | flops 13312 | bytes 104448 | tf_op jit(solution)/shard_map/psum | solution.py:250
  589.9 29.4 %reduce-scatter.3.cloned.1.call-done = bf16[256,5120]{1,0:T(8,128)(2,1)} async-done(((bf16[1024,5120]{1,0:T(8,128)(2,1)}), bf16[256,5120]{1,0:T(8,128)(2,1)}) %reduce-scatter.3.cloned.1.call-update) | async-done | bytes 2621456 | tf_op jit(solution)/shard_map/reduce_scatter | solution.py:232
  619.3 267.7 %all-reduce.6 = f32[256,5120]{1,0:T(8,128)} all-reduce(bf16[256,5120]{1,0:T(8,128)(2,1)} %reduce-scatter.3.cloned.1.call-done), channel_id=1, replica_groups=mesh['dp'=8,'seq'=4] {'dp'}, use_global_device_ids=true, to_apply=%region_17.18 | all-reduce | flops 1310720 | bytes 7864320 | tf_op jit(solution)/shard_map/psum | solution.py:238
  887.0 5.0 fusion.54
  892.0 114.9 %all-reduce.5.cloned.1.call-done = (f32[1024,1024]{0,1:T(8,128)}, f32[1024,1024]{0,1:T(8,128)}) async-done(((f32[1024,1024]{0,1:T(8,128)}, f32[1024,1024]{0,1:T(8,128)}), (f32[1024,1024]{0,1:T(8,128)}, f32[1024,1024]{0,1:T(8,128)})) %all-reduce.5.cloned.1.call-update) | async-done | bytes 8388624 | tf_op jit(solution)/shard_map/psum | solution.py:238
  1006.9 5.3 copy.88
  1012.3 5.3 copy.89
  (242 shorter events, 133.4 us)
Async XLA Ops:
  7.2 27.7 %copy-start.22 = (bf16[1,1024]{1,0:T(2,128)(2,1)S(1)}, bf16[1,1024]{1,0:T(2,128)(2,1)}, u32[]{:S(2)}) copy-start(bf16[1,1024]{1,0:T(2,128)(2,1)} %param.26) | copy-start | bytes 6148
  7.2 29.7 %copy-start.27 = (bf16[1024]{0:T(1024)(128)(2,1)S(1)}, bf16[1024]{0:T(1024)(128)(2,1)}, u32[]{:S(2)}) copy-start(bf16[1024]{0:T(1024)(128)(2,1)} %param.39) | copy-start | bytes 6148
  7.2 51.9 %copy-start.12 = (bf16[512,1024]{1,0:T(8,128)(2,1)S(1)}, bf16[512,1024]{1,0:T(8,128)(2,1)}, u32[]{:S(2)}) copy-start(bf16[512,1024]{1,0:T(8,128)(2,1)} %param.25) | copy-start | bytes 3145732
  7.2 27.7 %all-gather.8.cloned.1.call-start = ((), (), s32[]{:S(2)}) async-start(), calls=%async_computation.6 | async-start | bytes 2621440 | tf_op jit(solution)/shard_map/all_gather | solution.py:122
  8.0 51.1 %all-gather.12.cloned.1.call-start = ((), (), s32[]{:S(2)}) async-start(), calls=%async_computation.8 | async-start | bytes 2621440 | tf_op jit(solution)/shard_map/all_gather | solution.py:119
  8.7 74.5 %all-gather.10.cloned.1.call-start = ((), (), s32[]{:S(2)}) async-start(), calls=%async_computation.7 | async-start | bytes 2621440 | tf_op jit(solution)/shard_map/all_gather | solution.py:118
  9.5 97.8 %all-gather.14.cloned.1.call-start = ((), (), s32[]{:S(2)}) async-start(), calls=%async_computation.9 | async-start | bytes 2621440 | tf_op jit(solution)/shard_map/all_gather | solution.py:120
  10.0 213.6 %all-gather.16.cloned.1.call-start = ((), (), s32[]{:S(2)}) async-start(), calls=%async_computation.10 | async-start | bytes 2621440 | tf_op jit(solution)/shard_map/all_gather | solution.py:121
  10.6 236.4 %all-gather.18.cloned.1.call-start = ((), (), s32[]{:S(2)}) async-start(), calls=%async_computation.11 | async-start | bytes 10485760 | tf_op jit(solution)/shard_map/all_gather | solution.py:123
  36.9 204.8 %copy-start.16 = (f32[1024]{0:T(1024)}, f32[1024]{0:T(1024)S(1)}, u32[]{:S(2)}) copy-start(f32[1024]{0:T(1024)S(1)} %convert_add_fusion.1) | copy-start | bytes 12292
  116.3 5.8 copy-start.37
  116.3 83.5 %all-to-all-start = ((bf16[1,512,3,1024]{1,2,0,3:T(4,128)(2,1)}), bf16[1,512,3,1024]{1,2,0,3:T(4,128)(2,1)}, u32[]{:S(2)}, u32[]{:S(2)}) async-start(bf16[1,512,3,1024]{1,2,0,3:T(4,128)(2,1)} %copy.80), calls=%async_computation | async-start | bytes 8388608 | tf_op jit(solution)/shard_map/all_to_all | solution.py:155
  121.4 163.1 %all-gather.20.cloned.1.call-start = ((), (), s32[]{:S(2)}) async-start(), calls=%async_computation.12 | async-start | bytes 10485760 | tf_op jit(solution)/shard_map/all_gather | solution.py:124
  202.8 20.7 %copy-start.28 = (bf16[1024]{0:T(1024)(128)(2,1)S(1)}, bf16[1024]{0:T(1024)(128)(2,1)}, u32[]{:S(2)}) copy-start(bf16[1024]{0:T(1024)(128)(2,1)} %param.38) | copy-start | bytes 6148
  202.8 20.7 %copy-start.29 = (bf16[1024]{0:T(1024)(128)(2,1)S(1)}, bf16[1024]{0:T(1024)(128)(2,1)}, u32[]{:S(2)}) copy-start(bf16[1024]{0:T(1024)(128)(2,1)} %param.42) | copy-start | bytes 6148
  202.8 20.7 %copy-start.30 = (bf16[1024]{0:T(1024)(128)(2,1)S(1)}, bf16[1024]{0:T(1024)(128)(2,1)}, u32[]{:S(2)}) copy-start(bf16[1024]{0:T(1024)(128)(2,1)} %param.43) | copy-start | bytes 6148
  202.8 20.7 %copy-start.24 = (bf16[4096]{0:T(1024)(128)(2,1)S(1)}, bf16[4096]{0:T(1024)(128)(2,1)}, u32[]{:S(2)}) copy-start(bf16[4096]{0:T(1024)(128)(2,1)} %param.40) | copy-start | bytes 24580
  202.8 20.7 %copy-start.31 = (bf16[1024]{0:T(1024)(128)(2,1)S(1)}, bf16[1024]{0:T(1024)(128)(2,1)}, u32[]{:S(2)}) copy-start(bf16[1024]{0:T(1024)(128)(2,1)} %param.41) | copy-start | bytes 6148
  202.9 20.7 %copy-start.32 = (bf16[1024]{0:T(1024)(128)(2,1)S(1)}, bf16[1024]{0:T(1024)(128)(2,1)}, u32[]{:S(2)}) copy-start(bf16[1024]{0:T(1024)(128)(2,1)} %param.44) | copy-start | bytes 6148
  202.9 20.7 %copy-start.33 = (bf16[1024]{0:T(1024)(128)(2,1)S(1)}, bf16[1024]{0:T(1024)(128)(2,1)}, u32[]{:S(2)}) copy-start(bf16[1024]{0:T(1024)(128)(2,1)} %param.45) | copy-start | bytes 6148
  219.2 4.3 copy-start.18
  219.2 22.5 %all-to-all-start.1 = ((bf16[4,512,256]{1,2,0:T(8,128)(2,1)}), bf16[4,512,256]{1,2,0:T(8,128)(2,1)}, u32[]{:S(2)}, u32[]{:S(2)}) async-start(bf16[4,512,256]{1,2,0:T(8,128)(2,1)} %get-tuple-element.79), calls=%async_computation.1 | async-start | bytes 2097152 | tf_op jit(solution)/shard_map/all_to_all | solution.py:157
  223.4 310.5 %reduce-scatter.5.cloned.1.call-start = ((), (), s32[]{:S(2)}) async-start(), calls=%async_computation.14 | async-start | bytes 20971520 | tf_op jit(solution)/shard_map/reduce_scatter | solution.py:220
  284.5 10.3 %copy-start.8 = (bf16[512,1024]{1,0:T(8,128)(2,1)S(1)}, bf16[512,1024]{1,0:T(8,128)(2,1)}, u32[]{:S(2)}) copy-start(bf16[512,1024]{1,0:T(8,128)(2,1)} %param.28) | copy-start | bytes 3145732
  307.7 13.5 %copy-start.1 = (f32[512,1024]{1,0:T(8,128)S(1)}, f32[512,1024]{1,0:T(8,128)}, u32[]{:S(2)}) copy-start(f32[512,1024]{1,0:T(8,128)} %copy-done) | copy-start | bytes 6291460
  321.2 7.0 copy-start.39
  342.2 11.4 %copy-start.2 = (f32[512,1024]{1,0:T(8,128)S(1)}, f32[512,1024]{1,0:T(8,128)}, u32[]{:S(2)}) copy-start(f32[512,1024]{1,0:T(8,128)} %copy-done) | copy-start | bytes 6291460
  378.8 30.4 %all-to-all-start.2 = ((bf16[4,2,65536]{2,1,0:T(2,128)(2,1)}), bf16[4,2,65536]{2,1,0:T(2,128)(2,1)}, u32[]{:S(2)}, u32[]{:S(2)}) async-start(bf16[4,2,65536]{2,1,0:T(2,128)(2,1)} %reshape.269), calls=%async_computation.2 | async-start | bytes 2097152 | tf_op jit(solution)/shard_map/all_to_all | solution.py:191
  451.1 59.6 %all-to-all-start.3 = ((bf16[4,512,3,256]{1,3,2,0:T(8,128)(2,1)}), bf16[4,512,3,256]{1,3,2,0:T(8,128)(2,1)S(1)}, u32[]{:S(2)}, u32[]{:S(2)}) async-start(bf16[4,512,3,256]{1,3,2,0:T(8,128)(2,1)} %get-tuple-element.81), calls=%async_computation.3 | async-start | bytes 6291456 | tf_op jit(solution)/shard_map/all_to_all | solution.py:199
  454.9 164.4 %reduce-scatter.3.cloned.1.call-start = ((), (), s32[]{:S(2)}) async-start(), calls=%async_computation.13 | async-start | bytes 13107200 | tf_op jit(solution)/shard_map/reduce_scatter | solution.py:232
  510.9 9.1 copy-start.3
  533.9 473.0 %all-reduce.5.cloned.1.call-start = ((), (), s32[]{:S(2)}) async-start(), calls=%async_computation.15 | async-start | bytes 16777216 | tf_op jit(solution)/shard_map/psum | solution.py:238
  (22 other events, 62.4 us)
Sparse Core Ops, SparseCore 0:
  9.6 25.2 all-gather.7
  36.5 22.5 all-gather.11
  60.7 22.5 all-gather.9
  84.7 22.5 all-gather.13
  108.7 27.7 all-gather.15
  137.9 83.4 all-gather.17
  223.0 61.5 all-gather.19
  342.3 155.0 reduce-scatter.4
  534.0 85.2 reduce-scatter.2
  624.4 382.4 all-reduce.4
where the time goes:
time: 1030 us; the launch traced here: 1020 us
  waiting for transfers between devices  419 us (41%)
  blocking collectives  309 us (30%)
  matrix products  135 us (13%)
  local copies, waits for them, and re-layouts  75.6 us (7%)
  other arithmetic  52.9 us (5%)
  starting transfers between devices  17.8 us (2%)
  between operations  15.3 us (1%)
    psum x1, blocking collectives, local(): lax.psum((share_in, share_down, attn_share), 'dp')  268 us
    psum x1, waiting for transfers between devices, local(): lax.psum((share_in, share_down, attn_share), 'dp')  115 us
    all_to_all x1, waiting for transfers between devices, local(): lax.all_to_all(stacked, 'seq', split_axis=3, concat_axis=0, tiled=True)  77.5 us
    all_to_all x1, waiting for transfers between devices, local(): lax.all_to_all(grad_stack, 'seq', split_axis=0, concat_axis=3, tiled=True)  51.5 us
    psum x1, blocking collectives, local(): lax.psum((jnp.sum(grad_query_rows, axis=0, dtype=jnp.float32), jnp.sum(gr...  41.3 us
    unnamed x86, local copies, waits for them, and re-layouts  32.8 us
    reduce_scatter x1, waiting for transfers between devices, local(): lax.psum_scatter(jnp.concatenate([term_qkv, term_out, term_time], axis=1)...  29.4 us
    dot_general x1, matrix products, local(): jnp.einsum('td,fd->tf', first_low, full_in, preferred_element_type=jnp.fl...  27.2 us
  transfers between devices with their start and end apart: 14, of which 11 were waited for; matrix products, arithmetic and copies ran while one was open for 18% of the time, Pallas kernels for 0%

commit v1 on v0

--- a/solution.py
+++ b/solution.py
@@ -7,6 +7,28 @@
 BLOCK = 25
 norm_eps = 1e-05
 neg_large = -1e30
+
+
+def joined_along(pieces, dim):
+    pieces = jnp.moveaxis(pieces, 0, dim)
+    shape = pieces.shape
+    return pieces.reshape(*shape[:dim], shape[dim] * shape[dim + 1], *shape[dim + 2 :])
+
+
+def gather_around(array, axis, dim):
+    size = lax.axis_size(axis)
+    pairs = [(i, (i + 1) % size) for i in range(size)]
+    back = [(b, a) for a, b in pairs]
+    lower, upper = ([], [])
+    for turn in range(size - 1):
+        if turn % 2 == 0:
+            lower.append(lax.ppermute(lower[-1] if lower else array, axis, pairs))
+        else:
+            upper.append(lax.ppermute(upper[-1] if upper else array, axis, back))
+    pieces = jnp.stack([*lower[::-1], array, *upper])
+    shift = lax.axis_index(axis) - len(lower)
+    pieces = pieces[(jnp.arange(size) - shift) % size]
+    return joined_along(pieces, dim)
 
 
 def layer_norm(values, gain, shift):
@@ -119,7 +141,7 @@
         lax.all_gather(w_key, "seq", axis=0, tiled=True),
         lax.all_gather(w_value, "seq", axis=0, tiled=True),
         lax.all_gather(w_out, "seq", axis=0, tiled=True),
-        lax.all_gather(w_time, "seq", axis=0, tiled=True),
+        gather_around(w_time, "seq", 0),
         lax.all_gather(w_in, "seq", axis=0, tiled=True),
         lax.all_gather(w_down, "seq", axis=0, tiled=True),
     )

time: 1030 us -> 1020 us (level)
  waiting for transfers between devices: 419 us -> 389 us
    all_gather x1 -> x0, waiting for transfers between devices: 23.7 us -> none  [local(): lax.all_gather(w_time, 'seq', axis=0, tiled=True)]
    ppermute x0 -> x3, waiting for transfers between devices: none -> 22.2 us  [the longest x2 22.2 us: gather_around(): lower.append(lax.ppermute(lower[-1] if lower else array, axis, pairs))]
    all_gather x1, waiting for transfers between devices: 22.2 us -> 0.02 us  [local(): lax.all_gather(w_key, 'seq', axis=0, tiled=True)]
    unnamed x86 -> x92, local copies, waits for them, and re-layouts: 32.8 us -> 34.2 us
  transfers between devices with their start and end apart: 14 -> 16, of which waited for: 11 -> 12; matrix products, arithmetic and copies ran while one was open for 18% -> 19% of each run, Pallas kernels for 0% -> 0%
where the time goes in v1:
time: 1020 us; the launch traced here: 1010 us
  waiting for transfers between devices  389 us (38%)
  blocking collectives  308 us (30%)
  matrix products  135 us (13%)
  local copies, waits for them, and re-layouts  79 us (8%)
  other arithmetic  54.4 us (5%)
  starting transfers between devices  27.3 us (3%)
  between operations  15 us (1%)
    psum x1, blocking collectives, local(): lax.psum((share_in, share_down, attn_share), 'dp')  266 us
    psum x1, waiting for transfers between devices, local(): lax.psum((share_in, share_down, attn_share), 'dp')  116 us
    all_to_all x1, waiting for transfers between devices, local(): lax.all_to_all(stacked, 'seq', split_axis=3, concat_axis=0, tiled=True)  77.7 us
    all_to_all x1, waiting for transfers between devices, local(): lax.all_to_all(grad_stack, 'seq', split_axis=0, concat_axis=3, tiled=True)  50.7 us
    psum x1, blocking collectives, local(): lax.psum((jnp.sum(grad_query_rows, axis=0, dtype=jnp.float32), jnp.sum(gr...  41.3 us
    unnamed x92, local copies, waits for them, and re-layouts  34.2 us
    reduce_scatter x1, waiting for transfers between devices, local(): lax.psum_scatter(jnp.concatenate([term_qkv, term_out, term_time], axis=1)...  29.4 us
    dot_general x1, matrix products, local(): jnp.einsum('td,fd->tf', first_low, full_in, preferred_element_type=jnp.fl...  27.2 us
  transfers between devices with their start and end apart: 16, of which 12 were waited for; matrix products, arithmetic and copies ran while one was open for 19% of the time, Pallas kernels for 0%

profile of v1, /device:TPU:0, one launch (start us, length us, event | category | flops | bytes accessed | tf_op | source)
XLA Modules:
  0.0 1008.2 jit_solution(9404630528829147486)
XLA Ops:
  13.2 10.6 %collective-permute-done = bf16[256,1024]{1,0:T(8,128)(2,1)S(1)} collective-permute-done((bf16[256,1024]{1,0:T(8,128)(2,1)S(1)}, bf16[256,1024]{1,0:T(8,128)(2,1)S(1)}, u32[]{:S(2)}, u32[]{:S(2)}) %collective-permute-start) | collective-permute-done | bytes 524320 | tf_op jit(solution)/shard_map/ppermute | solution.py:25
  23.8 7.0 collective-permute-start.1
  30.9 11.6 %collective-permute-done.1 = bf16[256,1024]{1,0:T(8,128)(2,1)S(1)} collective-permute-done((bf16[256,1024]{1,0:T(8,128)(2,1)S(1)}, bf16[256,1024]{1,0:T(8,128)(2,1)S(1)}, u32[]{:S(2)}, u32[]{:S(2)}) %collective-permute-start.1) | collective-permute-done | bytes 524320 | tf_op jit(solution)/shard_map/ppermute | solution.py:25
  52.6 14.3 %all-gather.7.cloned.1.call-done = bf16[1024,1024]{1,0:T(8,128)(2,1)} async-done(((bf16[256,1024]{1,0:T(8,128)(2,1)}), bf16[1024,1024]{1,0:T(8,128)(2,1)}) %all-gather.7.cloned.1.call-update) | async-done | bytes 2097168 | tf_op jit(solution)/shard_map/all_gather | solution.py:140
  70.7 20.3 %all-gather.11.cloned.1.call-done = bf16[1024,1024]{1,0:T(8,128)(2,1)} async-done(((bf16[256,1024]{1,0:T(8,128)(2,1)}), bf16[1024,1024]{1,0:T(8,128)(2,1)}) %all-gather.11.cloned.1.call-update) | async-done | bytes 2097168 | tf_op jit(solution)/shard_map/all_gather | solution.py:142
  94.4 5.7 copy.80
  100.1 5.1 all-to-all-start
  105.9 77.7 %all-to-all-done = bf16[1,512,3,1024]{1,2,0,3:T(4,128)(2,1)} async-done(((bf16[1,512,3,1024]{1,2,0,3:T(4,128)(2,1)}), bf16[1,512,3,1024]{1,2,0,3:T(4,128)(2,1)}, u32[]{:S(2)}, u32[]{:S(2)}) %all-to-all-start) | async-done | bytes 3145760 | tf_op jit(solution)/shard_map/all_to_all | solution.py:177
  186.7 16.3 %while.22 = (s32[]{:T(128)}, bf16[4,512,256]{1,2,0:T(8,128)(2,1)}, f32[4,4,512]{2,1,0:T(4,128)S(1)}, bf16[4,512,3,256]{1,3,2,0:T(8,128)(2,1)S(1)}, pred[4,512]{1,0:T(4,128)(4,1)S(1)}, /*index=5*/s32[]{:T(128)}) while((s32[]{:T(128)}, bf16[4,512,256]{1,2,0:T(8,128)(2,1)}, f32[4,4,512]{2,1,0:T(4,128)S(1)}, ...), condition=%wide.region_3.4_spmd, body=%wide.region_0.3_spmd.sunk | while | flops 281147392 | bytes 17370192 | solution.py:178
  207.5 18.2 %all-to-all-done.1 = bf16[4,512,256]{1,2,0:T(8,128)(2,1)} async-done(((bf16[4,512,256]{1,2,0:T(8,128)(2,1)}), bf16[4,512,256]{1,2,0:T(8,128)(2,1)}, u32[]{:S(2)}, u32[]{:S(2)}) %all-to-all-start.1) | async-done | bytes 1048608 | tf_op jit(solution)/shard_map/all_to_all | solution.py:179
  231.0 27.2 %multiply_convert_fusion.1 = (bf16[512,4096]{1,0:T(8,128)(2,1)}, f32[512,4096]{1,0:T(8,128)}, f32[512,4096]{1,0:T(8,128)}) fusion(f32[4096]{0:T(1024)S(1)} %convert_element_type.170, bf16[4096,1024]{1,0:T(8,128)(2,1)} %all-gather.15.cloned.1.call-done, f32[512,1024]{1,0:T(8,128)} %copy-done, f32[1024]{0:T(1024)S(1)} %convert_element_type.168, ...), kind=kOutput, calls=%fused_computation.38 | convolution fusion | flops 4436000768 | bytes 31485952 | tf_op jit(solution)/shard_map/td,fd->tf/dot_general | solution.py:186
  258.2 10.2 %all-gather.17.cloned.1.call-done = bf16[4096,1024]{1,0:T(8,128)(2,1)} async-done(((bf16[1024,1024]{1,0:T(8,128)(2,1)}), bf16[4096,1024]{1,0:T(8,128)(2,1)}) %all-gather.17.cloned.1.call-update) | async-done | bytes 8388624 | tf_op jit(solution)/shard_map/all_gather | solution.py:146
  268.4 10.0 fusion.61
  284.4 7.2 convolution_convert_fusion
  291.6 13.5 %convert_reduce_fusion = (f32[4096]{0:T(1024)S(1)}, bf16[512,4096]{1,0:T(8,128)(2,1)S(1)}) fusion(f32[512,4096]{1,0:T(8,128)} %get-tuple-element.209, f32[512,4096]{1,0:T(8,128)} %get-tuple-element.234, f32[4096]{0:T(1024)S(1)} %convert_element_type.170, bf16[512,1024]{1,0:T(8,128)(2,1)S(1)} %get-tuple-element.199, ...), kind=kOutput, calls=%fused_computation.36 | convolution fusion | flops 4330614784 | bytes 30441472 | tf_op jit(solution)/shard_map/td,fd->tf/dot_general | solution.py:205
  305.1 7.0 convolution_convert_fusion.1
  312.1 13.8 %pad_maximum_fusion = bf16[4096,2048]{0,1:T(8,128)(2,1)} fusion(bf16[4096,1024]{0,1:T(8,128)(2,1)} %convolution_convert_fusion, bf16[4096,1024]{0,1:T(8,128)(2,1)} %convolution_convert_fusion.1), kind=kLoop, calls=%fused_computation.32 | loop fusion | flops 33554432 | bytes 33554432 | tf_op jit(solution)/shard_map/concatenate | solution.py:243
  326.0 11.4 %multiply_reduce_fusion.2 = (f32[1024]{0:T(1024)S(1)}, f32[512]{0:T(512)S(1)}, f32[1024]{0:T(1024)S(1)}, f32[512,1024]{1,0:T(8,128)S(1)}) fusion(f32[512,1024]{1,0:T(8,128)} %copy-done, f32[512]{0:T(512)S(1)} %fusion.42, f32[512]{0:T(512)S(1)} %broadcast_multiply_fusion.1, f32[1024]{0:T(1024)S(1)} %convert_element_type.167, ...), kind=kOutput, calls=%fused_computation.63 | convolution fusion | flops 4300207616 | bytes 18894848 | tf_op jit(solution)/shard_map/dot_general | solution.py:207
  343.6 6.2 copy.82
  350.3 9.0 reduce.7
  367.5 26.1 %all-to-all-done.2 = bf16[4,2,65536]{2,1,0:T(2,128)(2,1)} async-done(((bf16[4,2,65536]{2,1,0:T(2,128)(2,1)}), bf16[4,2,65536]{2,1,0:T(2,128)(2,1)}, u32[]{:S(2)}, u32[]{:S(2)}) %all-to-all-start.2) | async-done | bytes 1048608 | tf_op jit(solution)/shard_map/all_to_all | solution.py:213
  400.4 35.0 %while.23 = (s32[]{:T(128)}, bf16[4,512,3,256]{1,3,2,0:T(8,128)(2,1)}, bf16[4,512,3,256]{1,3,2,0:T(8,128)(2,1)S(1)}, pred[4,512]{1,0:T(4,128)(4,1)S(1)}, f32[4,4...) while((s32[]{:T(128)}, bf16[4,512,3,256]{1,3,2,0:T(8,128)(2,1)}, ...), condition=%wide.region_14.15_spmd, body=%wide.region_12.14_spmd.sunk | while | flops 689829888 | bytes 39382108 | solution.py:220
  443.7 50.7 %all-to-all-done.3 = bf16[4,512,3,256]{1,3,2,0:T(8,128)(2,1)S(1)} async-done(((bf16[4,512,3,256]{1,3,2,0:T(8,128)(2,1)}), bf16[4,512,3,256]{1,3,2,0:T(8,128)(2,1)S(1)}, u32[]{:S(2)}, u32[]{:S(2)}) %all-to-all-start.3) | async-done | bytes 3145760 | tf_op jit(solution)/shard_map/all_to_all | solution.py:221
  507.8 9.9 pad_maximum_fusion.1
  517.7 6.8 fusion.57
  532.4 41.3 %all-reduce = (f32[1024]{0:T(1024)}, f32[1024]{0:T(1024)}, f32[1024]{0:T(1024)}, f32[1024]{0:T(1024)}, f32[4096]{0:T(1024)}, /*index=5*/f32[1024]{0:T(1024)}, f3...) all-reduce(f32[1024]{0:T(1024)S(1)} %get-tuple-element.240, ...), channel_id=1, replica_groups=mesh['dp'=8,'seq'=4] {'dp','seq'}, use_global_device_ids=true, to_apply=%region_22.23 | all-reduce | flops 13312 | bytes 104448 | tf_op jit(solution)/shard_map/psum | solution.py:272
  573.7 29.4 %reduce-scatter.3.cloned.1.call-done = bf16[256,5120]{1,0:T(8,128)(2,1)} async-done(((bf16[1024,5120]{1,0:T(8,128)(2,1)}), bf16[256,5120]{1,0:T(8,128)(2,1)}) %reduce-scatter.3.cloned.1.call-update) | async-done | bytes 2621456 | tf_op jit(solution)/shard_map/reduce_scatter | solution.py:254
  603.1 266.3 %all-reduce.6 = f32[256,5120]{1,0:T(8,128)} all-reduce(bf16[256,5120]{1,0:T(8,128)(2,1)} %reduce-scatter.3.cloned.1.call-done), channel_id=1, replica_groups=mesh['dp'=8,'seq'=4] {'dp'}, use_global_device_ids=true, to_apply=%region_17.18 | all-reduce | flops 1310720 | bytes 7864320 | tf_op jit(solution)/shard_map/psum | solution.py:260
  869.4 5.0 fusion.56
  874.4 116.1 %all-reduce.5.cloned.1.call-done = (f32[1024,1024]{0,1:T(8,128)}, f32[1024,1024]{0,1:T(8,128)}) async-done(((f32[1024,1024]{0,1:T(8,128)}, f32[1024,1024]{0,1:T(8,128)}), (f32[1024,1024]{0,1:T(8,128)}, f32[1024,1024]{0,1:T(8,128)})) %all-reduce.5.cloned.1.call-update) | async-done | bytes 8388624 | tf_op jit(solution)/shard_map/psum | solution.py:260
  990.6 5.3 copy.88
  995.9 5.3 copy.89
  (255 shorter events, 144.6 us)
Async XLA Ops:
  7.2 23.5 %copy-start.28 = (bf16[1024]{0:T(1024)(128)(2,1)S(1)}, bf16[1024]{0:T(1024)(128)(2,1)}, u32[]{:S(2)}) copy-start(bf16[1024]{0:T(1024)(128)(2,1)} %param.36) | copy-start | bytes 6148
  7.2 23.5 %copy-start.29 = (bf16[1024]{0:T(1024)(128)(2,1)S(1)}, bf16[1024]{0:T(1024)(128)(2,1)}, u32[]{:S(2)}) copy-start(bf16[1024]{0:T(1024)(128)(2,1)} %param.37) | copy-start | bytes 6148
  7.2 41.5 %all-gather.9.cloned.1.call-start = ((), (), s32[]{:S(2)}) async-start(), calls=%async_computation.7 | async-start | bytes 2621440 | tf_op jit(solution)/shard_map/all_gather | solution.py:141
  8.0 58.9 %all-gather.7.cloned.1.call-start = ((), (), s32[]{:S(2)}) async-start(), calls=%async_computation.6 | async-start | bytes 2621440 | tf_op jit(solution)/shard_map/all_gather | solution.py:140
  8.7 82.4 %all-gather.11.cloned.1.call-start = ((), (), s32[]{:S(2)}) async-start(), calls=%async_computation.8 | async-start | bytes 2621440 | tf_op jit(solution)/shard_map/all_gather | solution.py:142
  9.4 198.1 %all-gather.13.cloned.1.call-start = ((), (), s32[]{:S(2)}) async-start(), calls=%async_computation.9 | async-start | bytes 2621440 | tf_op jit(solution)/shard_map/all_gather | solution.py:143
  10.0 221.0 %all-gather.15.cloned.1.call-start = ((), (), s32[]{:S(2)}) async-start(), calls=%async_computation.10 | async-start | bytes 10485760 | tf_op jit(solution)/shard_map/all_gather | solution.py:145
  10.6 13.1 %collective-permute-start = (bf16[256,1024]{1,0:T(8,128)(2,1)S(1)}, bf16[256,1024]{1,0:T(8,128)(2,1)S(1)}, u32[]{:S(2)}, u32[]{:S(2)}) collective-permute-start(bf16[256,1024]{1,0:T(8,128)(2,1)S(1)} %copy-done.16), channel_id=1, source_target_pairs={{0,1},{1,2},{2,3},{3,0},{4,5},{5,6},{6,7},{7,4},{8,9},{9,10},{10,1... | collective-permute-start | bytes 1572872 | tf_op jit(solution)/shard_map/ppermute | solution.py:25
  11.2 19.7 %collective-permute-start.2 = (bf16[256,1024]{1,0:T(8,128)(2,1)S(1)}, bf16[256,1024]{1,0:T(8,128)(2,1)S(1)}, u32[]{:S(2)}, u32[]{:S(2)}) collective-permute-start(bf16[256,1024]{1,0:T(8,128)(2,1)S(1)} %copy-done.16), channel_id=1, source_target_pairs={{1,0},{2,1},{3,2},{0,3},{5,4},{6,5},{7,6},{4,7},{9,8},{10,9},{11,1... | collective-permute-start | bytes 1572872 | tf_op jit(solution)/shard_map/ppermute | solution.py:27
  23.8 18.7 %collective-permute-start.1 = (bf16[256,1024]{1,0:T(8,128)(2,1)S(1)}, bf16[256,1024]{1,0:T(8,128)(2,1)S(1)}, u32[]{:S(2)}, u32[]{:S(2)}) collective-permute-start(bf16[256,1024]{1,0:T(8,128)(2,1)S(1)} %collective-permute-done), channel_id=1, source_target_pairs={{0,1},{1,2},{2,3},{3,0},{4,5},{5,6},{6,7},{7,4},{8,9},{9,10},{10,1... | collective-permute-start | bytes 1572872 | tf_op jit(solution)/shard_map/ppermute | solution.py:25
  30.9 11.6 %copy-start.17 = (bf16[256,1024]{1,0:T(8,128)(2,1)}, bf16[256,1024]{1,0:T(8,128)(2,1)S(1)}, u32[]{:S(2)}) copy-start(bf16[256,1024]{1,0:T(8,128)(2,1)S(1)} %collective-permute-done.2) | copy-start | bytes 1572868
  48.7 177.0 %copy-start.19 = (f32[1024]{0:T(1024)}, f32[1024]{0:T(1024)S(1)}, u32[]{:S(2)}) copy-start(f32[1024]{0:T(1024)S(1)} %convert_add_fusion.1) | copy-start | bytes 12292
  100.1 83.5 %all-to-all-start = ((bf16[1,512,3,1024]{1,2,0,3:T(4,128)(2,1)}), bf16[1,512,3,1024]{1,2,0,3:T(4,128)(2,1)}, u32[]{:S(2)}, u32[]{:S(2)}) async-start(bf16[1,512,3,1024]{1,2,0,3:T(4,128)(2,1)} %copy.80), calls=%async_computation | async-start | bytes 8388608 | tf_op jit(solution)/shard_map/all_to_all | solution.py:177
  105.2 163.2 %all-gather.17.cloned.1.call-start = ((), (), s32[]{:S(2)}) async-start(), calls=%async_computation.11 | async-start | bytes 10485760 | tf_op jit(solution)/shard_map/all_gather | solution.py:146
  186.6 20.7 %copy-start.31 = (bf16[1024]{0:T(1024)(128)(2,1)S(1)}, bf16[1024]{0:T(1024)(128)(2,1)}, u32[]{:S(2)}) copy-start(bf16[1024]{0:T(1024)(128)(2,1)} %param.38) | copy-start | bytes 6148
  186.6 20.7 %copy-start.32 = (bf16[1024]{0:T(1024)(128)(2,1)S(1)}, bf16[1024]{0:T(1024)(128)(2,1)}, u32[]{:S(2)}) copy-start(bf16[1024]{0:T(1024)(128)(2,1)} %param.42) | copy-start | bytes 6148
  186.6 20.7 %copy-start.33 = (bf16[1024]{0:T(1024)(128)(2,1)S(1)}, bf16[1024]{0:T(1024)(128)(2,1)}, u32[]{:S(2)}) copy-start(bf16[1024]{0:T(1024)(128)(2,1)} %param.43) | copy-start | bytes 6148
  186.7 20.7 %copy-start.27 = (bf16[4096]{0:T(1024)(128)(2,1)S(1)}, bf16[4096]{0:T(1024)(128)(2,1)}, u32[]{:S(2)}) copy-start(bf16[4096]{0:T(1024)(128)(2,1)} %param.40) | copy-start | bytes 24580
  186.7 20.7 %copy-start.34 = (bf16[1024]{0:T(1024)(128)(2,1)S(1)}, bf16[1024]{0:T(1024)(128)(2,1)}, u32[]{:S(2)}) copy-start(bf16[1024]{0:T(1024)(128)(2,1)} %param.41) | copy-start | bytes 6148
  186.7 20.8 %copy-start.35 = (bf16[1024]{0:T(1024)(128)(2,1)S(1)}, bf16[1024]{0:T(1024)(128)(2,1)}, u32[]{:S(2)}) copy-start(bf16[1024]{0:T(1024)(128)(2,1)} %param.44) | copy-start | bytes 6148
  186.7 20.8 %copy-start.36 = (bf16[1024]{0:T(1024)(128)(2,1)S(1)}, bf16[1024]{0:T(1024)(128)(2,1)}, u32[]{:S(2)}) copy-start(bf16[1024]{0:T(1024)(128)(2,1)} %param.45) | copy-start | bytes 6148
  203.0 22.7 %all-to-all-start.1 = ((bf16[4,512,256]{1,2,0:T(8,128)(2,1)}), bf16[4,512,256]{1,2,0:T(8,128)(2,1)}, u32[]{:S(2)}, u32[]{:S(2)}) async-start(bf16[4,512,256]{1,2,0:T(8,128)(2,1)} %get-tuple-element.79), calls=%async_computation.1 | async-start | bytes 2097152 | tf_op jit(solution)/shard_map/all_to_all | solution.py:179
  207.3 310.5 %reduce-scatter.5.cloned.1.call-start = ((), (), s32[]{:S(2)}) async-start(), calls=%async_computation.13 | async-start | bytes 20971520 | tf_op jit(solution)/shard_map/reduce_scatter | solution.py:242
  268.4 10.3 %copy-start.8 = (bf16[512,1024]{1,0:T(8,128)(2,1)S(1)}, bf16[512,1024]{1,0:T(8,128)(2,1)}, u32[]{:S(2)}) copy-start(bf16[512,1024]{1,0:T(8,128)(2,1)} %param.28) | copy-start | bytes 3145732
  291.6 13.5 %copy-start.1 = (f32[512,1024]{1,0:T(8,128)S(1)}, f32[512,1024]{1,0:T(8,128)}, u32[]{:S(2)}) copy-start(f32[512,1024]{1,0:T(8,128)} %copy-done) | copy-start | bytes 6291460
  305.1 7.0 copy-start.42
  326.0 11.4 %copy-start.2 = (f32[512,1024]{1,0:T(8,128)S(1)}, f32[512,1024]{1,0:T(8,128)}, u32[]{:S(2)}) copy-start(f32[512,1024]{1,0:T(8,128)} %copy-done) | copy-start | bytes 6291460
  363.2 30.4 %all-to-all-start.2 = ((bf16[4,2,65536]{2,1,0:T(2,128)(2,1)}), bf16[4,2,65536]{2,1,0:T(2,128)(2,1)}, u32[]{:S(2)}, u32[]{:S(2)}) async-start(bf16[4,2,65536]{2,1,0:T(2,128)(2,1)} %reshape.330), calls=%async_computation.2 | async-start | bytes 2097152 | tf_op jit(solution)/shard_map/all_to_all | solution.py:213
  435.5 59.0 %all-to-all-start.3 = ((bf16[4,512,3,256]{1,3,2,0:T(8,128)(2,1)}), bf16[4,512,3,256]{1,3,2,0:T(8,128)(2,1)S(1)}, u32[]{:S(2)}, u32[]{:S(2)}) async-start(bf16[4,512,3,256]{1,3,2,0:T(8,128)(2,1)} %get-tuple-element.81), calls=%async_computation.3 | async-start | bytes 6291456 | tf_op jit(solution)/shard_map/all_to_all | solution.py:221
  439.3 163.8 %reduce-scatter.3.cloned.1.call-start = ((), (), s32[]{:S(2)}) async-start(), calls=%async_computation.12 | async-start | bytes 13107200 | tf_op jit(solution)/shard_map/reduce_scatter | solution.py:254
  494.6 9.1 copy-start.3
  517.7 472.9 %all-reduce.5.cloned.1.call-start = ((), (), s32[]{:S(2)}) async-start(), calls=%async_computation.14 | async-start | bytes 16777216 | tf_op jit(solution)/shard_map/psum | solution.py:260
  (27 other events, 78.5 us)
Sparse Core Ops, SparseCore 0:
  9.6 32.9 all-gather.8
  44.2 22.6 all-gather.6
  68.5 22.5 all-gather.10
  92.5 27.7 all-gather.12
  121.7 83.4 all-gather.14
  206.6 61.7 all-gather.16
  326.1 154.4 reduce-scatter.4
  517.8 85.2 reduce-scatter.2
  608.3 382.1 all-reduce.4
